TPU v7x, 32 devices: a whole 2x2x4 slice. The times are simulated.
32 devices in a mesh: row: 8 (over z, y), col: 4 (over x, core).
Axes of the slice: x: 2, y: 2, z: 4, core: 2. Of those that a mesh axis runs over, the one named last changes fastest.
Arguments:
- weights: bfloat16 [2, 8192, 8192], P(None, 'row', 'col'), may hold values from -0.0625 to 0.0625
- preact: float32 [2, 2, 8192], P(None, None, 'row'), may hold values from -2.5 to 2.5
- panel: bfloat16 [2, 64, 8192], P(None, None, 'col'), may hold values from -6 to 6
Outputs:
- basis_out: float32 [2, 64, 8192], P(None, None, 'col')
All inputs are finite; a program needn't handle non-finite values.
Results may differ from a plain program's by a relative error of at most 0.035.
Values may be sent and summed in bfloat16 or wider, within the bound.
A program may use at most 64 MiB of HBM per device.

v0:
```python
from functools import partial
import jax
import jax.numpy as jnp
from jax import lax
from jax.sharding import PartitionSpec as P

WIDTH = 8192
ITERS = 2


def on_device(weights, preact, panel):
    slopes = 1.0 - jnp.tanh(preact) ** 2
    layers = weights.shape[0]
    current = panel
    basis_out = panel.astype(jnp.float32)
    for iteration in range(ITERS):
        cotangent = None
        for layer_at in range(layers):
            partial_out = jnp.einsum(
                "bki,oi->bko", current, weights[layer_at], preferred_element_type=jnp.float32
            )
            summed = lax.psum_scatter(
                partial_out.astype(jnp.bfloat16), "col", scatter_dimension=1, tiled=True
            ).astype(jnp.float32)
            scaled = (slopes[:, layer_at, None, :] * summed).astype(jnp.bfloat16)
            if layer_at + 1 < layers:
                spread = lax.all_gather(scaled, "row", axis=2, tiled=True)
                current = lax.all_to_all(spread, "col", split_axis=2, concat_axis=1, tiled=True)
            else:
                cotangent = lax.all_gather(scaled, "col", axis=1, tiled=True)
        image_panel = None
        for layer_at in reversed(range(layers)):
            weighted = (slopes[:, layer_at, None, :] * cotangent).astype(jnp.bfloat16)
            partial_in = jnp.einsum(
                "bko,oi->bki", weighted, weights[layer_at], preferred_element_type=jnp.float32
            )
            if layer_at == 0:
                pieces = lax.psum_scatter(
                    partial_in.astype(jnp.bfloat16), "row", scatter_dimension=2, tiled=True
                )
                image_panel = lax.all_gather(pieces, "row", axis=2, tiled=True)
            else:
                pieces = lax.psum_scatter(
                    partial_in.astype(jnp.bfloat16), "row", scatter_dimension=1, tiled=True
                )
                spread = lax.all_gather(pieces, "col", axis=2, tiled=True)
                cotangent = lax.all_to_all(spread, "row", split_axis=2, concat_axis=1, tiled=True)
        local_gram = jnp.einsum(
            "bkw,bjw->bkj", image_panel, image_panel, preferred_element_type=jnp.float32
        )
        gram_sum = lax.psum(local_gram.astype(jnp.bfloat16), "col").astype(jnp.float32)
        factor = jnp.linalg.cholesky(gram_sum / WIDTH)
        basis_out = jax.vmap(partial(jax.scipy.linalg.solve_triangular, lower=True))(
            factor, image_panel.astype(jnp.float32)
        )
        current = basis_out.astype(jnp.bfloat16)
    return basis_out


def solution(mesh):
    return jax.shard_map(
        on_device,
        mesh=mesh,
        in_specs=(P(None, "row", "col"), P(None, None, "row"), P(None, None, "col")),
        out_specs=P(None, None, "col"),
        check_vma=False,
    )
```

profile of v0, /device:TPU:0, one launch (start us, length us, event | category | flops | bytes accessed | tf_op | source)
XLA Modules:
  0.0 776.8 jit_solution(17862595918340202358)
XLA Ops:
  6.5 1.0 copy-done
  7.6 4.4 fusion.40
  12.1 22.8 %reduce-scatter.13.cloned.1.call-done = bf16[2,16,1024]{2,1,0:T(8,128)(2,1)} async-done(((bf16[2,64,1024]{2,1,0:T(8,128)(2,1)}), bf16[2,16,1024]{2,1,0:T(8,128)(2,1)}) %reduce-scatter.13.cloned.1.call-update) | async-done | bytes 65552 | tf_op jit(solution)/shard_map/reduce_scatter | solution.py:22
  34.9 0.9 multiply_convert_fusion.7
  35.8 31.6 %all_gather.24 = bf16[2,16,8192]{2,1,0:T(8,128)(2,1)S(1)} all-gather(bf16[2,16,1024]{2,1,0:T(8,128)(2,1)S(1)} %multiply_convert_fusion.7), channel_id=1, replica_groups=mesh['row'=8,'col'=4] {'row'}, dimensions={2}, use_global_device_ids=true | all-gather | bytes 589824 | tf_op jit(solution)/shard_map/all_gather | solution.py:27
  67.4 6.7 copy.47
  74.1 5.8 reshape.23
  79.9 11.2 %all_to_all.54 = bf16[4,2,32768]{2,1,0:T(2,128)(2,1)S(1)} all-to-all(bf16[4,2,32768]{2,1,0:T(2,128)(2,1)S(1)} %reshape.23), channel_id=1, replica_groups=mesh['row'=8,'col'=4] {'col'}, dimensions={0} | all-to-all | bytes 1048576 | tf_op jit(solution)/shard_map/all_to_all | solution.py:28
  91.1 4.1 reshape.24
  95.2 9.7 %copy.67 = bf16[2,16,4,2048]{3,2,1,0:T(4,128)(2,1)S(1)} copy(bf16[2,16,4,2048]{1,0,3,2:T(2,128)(2,1)} %bitcast.105) | data formatting | bytes 1048576 | tf_op jit(solution)/shard_map/all_to_all | solution.py:28
  105.2 4.4 fusion.46
  109.7 20.0 %reduce-scatter.15.cloned.1.call-done = bf16[2,16,1024]{2,1,0:T(8,128)(2,1)} async-done(((bf16[2,64,1024]{2,1,0:T(8,128)(2,1)}), bf16[2,16,1024]{2,1,0:T(8,128)(2,1)}) %reduce-scatter.15.cloned.1.call-update) | async-done | bytes 65552 | tf_op jit(solution)/shard_map/reduce_scatter | solution.py:22
  129.8 0.9 multiply_convert_fusion.6
  130.6 5.8 all_gather.25
  136.4 2.9 fusion.34
  139.9 1.0 copy.75
  140.9 63.2 %reduce-scatter.25.cloned.1.call-done = bf16[8,4096]{1,0:T(8,128)(2,1)} async-done(((bf16[64,4096]{1,0:T(8,128)(2,1)}), bf16[8,4096]{1,0:T(8,128)(2,1)}) %reduce-scatter.25.cloned.1.call-update) | async-done | bytes 65552
  204.0 0.9 reshape.20
  204.9 5.8 all_gather.26
  210.7 6.7 copy.50
  217.4 6.4 reshape.25
  223.8 3.6 all-to-all-start.1
  227.8 9.0 %all-to-all-done.1 = bf16[8,2,8192]{2,1,0:T(2,128)(2,1)S(1)} async-done(((bf16[8,2,8192]{2,1,0:T(2,128)(2,1)}), bf16[8,2,8192]{2,1,0:T(2,128)(2,1)S(1)}, u32[]{:S(2)}, u32[]{:S(2)}) %all-to-all-start.1) | async-done | bytes 262176 | tf_op jit(solution)/shard_map/all_to_all | solution.py:47
  236.9 5.9 reshape.26
  242.8 7.5 fusion.2
  250.3 8.9 %copy.51 = bf16[2,8,8,1024]{3,2,1,0:T(8,128)(2,1)S(1)} copy(bf16[2,8,8,1024]{2,0,3,1:T(2,128)(2,1)} %fusion.2) | data formatting | bytes 524288 | tf_op jit(solution)/shard_map/convert_element_type | solution.py:33
  259.2 3.7 fusion.28
  263.0 62.1 %reduce-scatter.17.cloned.1.call-done = bf16[2,64,256]{2,1,0:T(8,128)(2,1)} async-done(((bf16[2,64,2048]{2,1,0:T(8,128)(2,1)}), bf16[2,64,256]{2,1,0:T(8,128)(2,1)}) %reduce-scatter.17.cloned.1.call-update) | async-done | bytes 65552 | tf_op jit(solution)/shard_map/reduce_scatter | solution.py:38
  325.1 31.8 %all_gather.27 = bf16[2,64,2048]{2,1,0:T(8,128)(2,1)S(1)} all-gather(bf16[2,64,256]{2,1,0:T(8,128)(2,1)} %reduce-scatter.17.cloned.1.call-done), channel_id=1, replica_groups=mesh['row'=8,'col'=4] {'row'}, dimensions={2}, use_global_device_ids=true | all-gather | bytes 589824 | tf_op jit(solution)/shard_map/all_gather | solution.py:41
  357.2 10.3 %psum.14 = bf16[2,64,64]{1,2,0:T(8,128)(2,1)S(1)} all-reduce(bf16[2,64,64]{1,2,0:T(8,128)(2,1)S(1)} %convolution_convert_fusion.2), channel_id=1, replica_groups=mesh['row'=8,'col'=4] {'col'}, use_global_device_ids=true, to_apply=%region_4.0 | all-reduce | flops 8192 | bytes 32768 | tf_op jit(solution)/shard_map/psum | solution.py:51
  367.6 11.7 %custom-call.8 = f32[2,64,64]{2,1,0:T(8,128)S(1)} custom-call(f32[2,64,64]{2,1,0:T(8,128)S(1)} %fusion.62), custom_call_target="Cholesky" | custom-call | tf_op jit(solution)/shard_map/jit(cholesky)/cholesky | solution.py:52
  379.6 9.8 %custom-call.9 = f32[2,1,64,64]{2,3,1,0:T(8,128)S(1)} custom-call(f32[2,1,64,64]{3,2,1,0:T(8,128)S(1)} %select_bitcast_fusion.1), custom_call_target="InvertDiagBlocksLowerTriangular" | custom-call | tf_op jit(solution)/shard_map/vmap(jit(_solve_triangular))/triangular_solve | solution.py:53
  389.4 1.1 convolution_convert_fusion
  390.5 4.4 fusion.43
  395.0 19.1 %reduce-scatter.19.cloned.1.call-done = bf16[2,16,1024]{2,1,0:T(8,128)(2,1)} async-done(((bf16[2,64,1024]{2,1,0:T(8,128)(2,1)}), bf16[2,16,1024]{2,1,0:T(8,128)(2,1)}) %reduce-scatter.19.cloned.1.call-update) | async-done | bytes 65552 | tf_op jit(solution)/shard_map/reduce_scatter | solution.py:22
  414.0 0.9 multiply_convert_fusion.5
  414.9 31.5 %all_gather.28 = bf16[2,16,8192]{2,1,0:T(8,128)(2,1)S(1)} all-gather(bf16[2,16,1024]{2,1,0:T(8,128)(2,1)S(1)} %multiply_convert_fusion.5), channel_id=1, replica_groups=mesh['row'=8,'col'=4] {'row'}, dimensions={2}, use_global_device_ids=true | all-gather | bytes 589824 | tf_op jit(solution)/shard_map/all_gather | solution.py:27
  446.4 6.7 copy.55
  453.1 5.8 reshape.27
  458.8 11.2 %all_to_all.55 = bf16[4,2,32768]{2,1,0:T(2,128)(2,1)S(1)} all-to-all(bf16[4,2,32768]{2,1,0:T(2,128)(2,1)S(1)} %reshape.27), channel_id=1, replica_groups=mesh['row'=8,'col'=4] {'col'}, dimensions={0} | all-to-all | bytes 1048576 | tf_op jit(solution)/shard_map/all_to_all | solution.py:28
  470.0 4.1 reshape.28
  474.2 9.7 %copy.68 = bf16[2,16,4,2048]{3,2,1,0:T(4,128)(2,1)S(1)} copy(bf16[2,16,4,2048]{1,0,3,2:T(2,128)(2,1)} %bitcast.107) | data formatting | bytes 1048576 | tf_op jit(solution)/shard_map/all_to_all | solution.py:28
  484.1 4.4 fusion.49
  488.7 20.2 %reduce-scatter.21.cloned.1.call-done = bf16[2,16,1024]{2,1,0:T(8,128)(2,1)} async-done(((bf16[2,64,1024]{2,1,0:T(8,128)(2,1)}), bf16[2,16,1024]{2,1,0:T(8,128)(2,1)}) %reduce-scatter.21.cloned.1.call-update) | async-done | bytes 65552 | tf_op jit(solution)/shard_map/reduce_scatter | solution.py:22
  508.9 0.9 multiply_convert_fusion.4
  509.7 5.8 all_gather.29
  515.5 2.9 fusion.37
  519.0 1.0 copy.76
  520.0 63.2 %reduce-scatter.27.cloned.1.call-done = bf16[8,4096]{1,0:T(8,128)(2,1)} async-done(((bf16[64,4096]{1,0:T(8,128)(2,1)}), bf16[8,4096]{1,0:T(8,128)(2,1)}) %reduce-scatter.27.cloned.1.call-update) | async-done | bytes 65552
  583.2 0.9 reshape.22
  584.1 5.8 all_gather.30
  589.9 6.7 copy.58
  596.6 5.8 reshape.29
  602.3 12.8 %all_to_all.56 = bf16[8,2,8192]{2,1,0:T(2,128)(2,1)S(1)} all-to-all(bf16[8,2,8192]{2,1,0:T(2,128)(2,1)S(1)} %reshape.29), channel_id=1, replica_groups=mesh['row'=8,'col'=4] {'row'}, dimensions={0} | all-to-all | bytes 524288 | tf_op jit(solution)/shard_map/all_to_all | solution.py:47
  615.2 5.9 reshape.30
  621.1 7.5 fusion.3
  628.6 8.9 %copy.59 = bf16[2,8,8,1024]{3,2,1,0:T(8,128)(2,1)S(1)} copy(bf16[2,8,8,1024]{2,0,3,1:T(2,128)(2,1)} %fusion.3) | data formatting | bytes 524288 | tf_op jit(solution)/shard_map/convert_element_type | solution.py:33
  637.5 3.8 fusion.31
  641.3 62.3 %reduce-scatter.23.cloned.1.call-done = bf16[2,64,256]{2,1,0:T(8,128)(2,1)} async-done(((bf16[2,64,2048]{2,1,0:T(8,128)(2,1)}), bf16[2,64,256]{2,1,0:T(8,128)(2,1)}) %reduce-scatter.23.cloned.1.call-update) | async-done | bytes 65552 | tf_op jit(solution)/shard_map/reduce_scatter | solution.py:38
  703.6 31.6 %all_gather.31 = bf16[2,64,2048]{2,1,0:T(8,128)(2,1)S(1)} all-gather(bf16[2,64,256]{2,1,0:T(8,128)(2,1)} %reduce-scatter.23.cloned.1.call-done), channel_id=1, replica_groups=mesh['row'=8,'col'=4] {'row'}, dimensions={2}, use_global_device_ids=true | all-gather | bytes 589824 | tf_op jit(solution)/shard_map/all_gather | solution.py:41
  735.5 10.5 %psum.15 = bf16[2,64,64]{1,2,0:T(8,128)(2,1)S(1)} all-reduce(bf16[2,64,64]{1,2,0:T(8,128)(2,1)S(1)} %convolution_convert_fusion.1), channel_id=1, replica_groups=mesh['row'=8,'col'=4] {'col'}, use_global_device_ids=true, to_apply=%region_11.14 | all-reduce | flops 8192 | bytes 32768 | tf_op jit(solution)/shard_map/psum | solution.py:51
  746.2 11.7 %custom-call.10 = f32[2,64,64]{2,1,0:T(8,128)S(1)} custom-call(f32[2,64,64]{2,1,0:T(8,128)S(1)} %fusion.60), custom_call_target="Cholesky" | custom-call | tf_op jit(solution)/shard_map/jit(cholesky)/cholesky | solution.py:52
  758.1 9.8 %custom-call.11 = f32[2,1,64,64]{2,3,1,0:T(8,128)S(1)} custom-call(f32[2,1,64,64]{3,2,1,0:T(8,128)S(1)} %select_bitcast_fusion), custom_call_target="InvertDiagBlocksLowerTriangular" | custom-call | tf_op jit(solution)/shard_map/vmap(jit(_solve_triangular))/triangular_solve | solution.py:53
  768.0 2.0 fusion.52
  (48 shorter events, 3.8 us)
Async XLA Ops:
  6.5 1.0 copy-start
  6.5 5.5 copy-start.2
  6.5 28.4 %reduce-scatter.13.cloned.1.call-start = ((), (), s32[]{:S(2)}) async-start(), calls=%async_computation.12 | async-start | bytes 327680 | tf_op jit(solution)/shard_map/reduce_scatter | solution.py:22
  12.0 117.8 %reduce-scatter.15.cloned.1.call-start = ((), (), s32[]{:S(2)}) async-start(), calls=%async_computation.13 | async-start | bytes 327680 | tf_op jit(solution)/shard_map/reduce_scatter | solution.py:22
  109.7 94.4 %reduce-scatter.25.cloned.1.call-start = ((), (), s32[]{:S(2)}) async-start(), calls=%async_computation.18 | async-start | bytes 589824
  223.8 13.1 %all-to-all-start.1 = ((bf16[8,2,8192]{2,1,0:T(2,128)(2,1)}), bf16[8,2,8192]{2,1,0:T(2,128)(2,1)S(1)}, u32[]{:S(2)}, u32[]{:S(2)}) async-start(bf16[8,2,8192]{2,1,0:T(2,128)(2,1)} %reshape.25), calls=%async_computation.3 | async-start | bytes 524288 | tf_op jit(solution)/shard_map/all_to_all | solution.py:47
  227.4 97.7 %reduce-scatter.17.cloned.1.call-start = ((), (), s32[]{:S(2)}) async-start(), calls=%async_computation.14 | async-start | bytes 589824 | tf_op jit(solution)/shard_map/reduce_scatter | solution.py:38
  262.9 151.1 %reduce-scatter.19.cloned.1.call-start = ((), (), s32[]{:S(2)}) async-start(), calls=%async_computation.15 | async-start | bytes 327680 | tf_op jit(solution)/shard_map/reduce_scatter | solution.py:22
  394.9 113.9 %reduce-scatter.21.cloned.1.call-start = ((), (), s32[]{:S(2)}) async-start(), calls=%async_computation.16 | async-start | bytes 327680 | tf_op jit(solution)/shard_map/reduce_scatter | solution.py:22
  488.6 94.6 %reduce-scatter.27.cloned.1.call-start = ((), (), s32[]{:S(2)}) async-start(), calls=%async_computation.19 | async-start | bytes 589824
  519.9 183.6 %reduce-scatter.23.cloned.1.call-start = ((), (), s32[]{:S(2)}) async-start(), calls=%async_computation.17 | async-start | bytes 589824 | tf_op jit(solution)/shard_map/reduce_scatter | solution.py:38
  637.5 132.5 %copy-start.1 = (bf16[2,64,2048]{2,1,0:T(8,128)(2,1)S(1)}, bf16[2,64,2048]{2,1,0:T(8,128)(2,1)}, u32[]{:S(2)}) copy-start(bf16[2,64,2048]{2,1,0:T(8,128)(2,1)} %param.8) | copy-start | bytes 1572868
Sparse Core Ops, SparseCore 0:
  12.1 22.7 reduce-scatter.12
  109.8 19.9 reduce-scatter.14
  141.0 63.0 reduce-scatter.24
  263.1 62.0 reduce-scatter.16
  395.0 18.9 reduce-scatter.18
  488.7 20.0 reduce-scatter.20
  520.1 63.1 reduce-scatter.26
  641.4 62.1 reduce-scatter.22
where the time goes:
time: 779 us; the launch traced here: 777 us
  waiting for transfers between devices  342 us (44%)
  blocking collectives  206 us (26%)
  local copies, waits for them, and re-layouts  114 us (15%)
  other arithmetic  62.1 us (8%)
  matrix products  34.7 us (4%)
  between operations  13.8 us (2%)
    unnamed x10, waiting for transfers between devices  127 us
    reduce_scatter x2, waiting for transfers between devices, on_device(): lax.psum_scatter(partial_in.astype(jnp.bfloat16), 'row', scatter_dimensio...  124 us
    reduce_scatter x4, waiting for transfers between devices, on_device(): lax.psum_scatter(partial_out.astype(jnp.bfloat16), 'col', scatter_dimensi...  82.1 us
    all_gather x2, blocking collectives, on_device(): image_panel = lax.all_gather(pieces, 'row', axis=2, tiled=True)  63.4 us
    all_gather x2, blocking collectives, on_device(): spread = lax.all_gather(scaled, 'row', axis=2, tiled=True)  63.1 us
    unnamed x24, local copies, waits for them, and re-layouts  49.6 us
    another operation x7, other arithmetic, on_device(): factor = jnp.linalg.cholesky(gram_sum / WIDTH)  23.8 us
    all_to_all x2, blocking collectives, on_device(): lax.all_to_all(spread, 'col', split_axis=2, concat_axis=1, tiled=True)  22.4 us
  transfers between devices with their start and end apart: 9, of which 9 were waited for; matrix products, arithmetic and copies ran while one was open for 0% of the time, Pallas kernels for 0%

commit v1 on v0

--- a/solution.py
+++ b/solution.py
@@ -24,7 +24,9 @@
             ).astype(jnp.float32)
             scaled = (slopes[:, layer_at, None, :] * summed).astype(jnp.bfloat16)
             if layer_at + 1 < layers:
-                spread = lax.all_gather(scaled, "row", axis=2, tiled=True)
+                spread = jnp.concatenate(
+                    lax.all_to_all(jnp.stack([scaled] * lax.axis_size("row")), "row", 0, 0), axis=2
+                )
                 current = lax.all_to_all(spread, "col", split_axis=2, concat_axis=1, tiled=True)
             else:
                 cotangent = lax.all_gather(scaled, "col", axis=1, tiled=True)

time: 779 us -> 753 us (0.967)
  blocking collectives: 206 us -> 182 us
    all_gather x2 -> x0, blocking collectives: 63.1 us -> none  [on_device(): spread = lax.all_gather(scaled, 'row', axis=2, tiled=True)]
    all_to_all x0 -> x2, blocking collectives: none -> 39.2 us  [on_device(): lax.all_to_all(jnp.stack([scaled] * lax.axis_size('row')), 'row', 0, 0)]
    reshape x0 -> x2, local copies, waits for them, and re-layouts: none -> 14.5 us  [on_device(): jnp.concatenate(lax.all_to_all(jnp.stack([scaled] * lax.axis_size('row'))...]
    all_gather x2 -> x0, local copies, waits for them, and re-layouts: 13.4 us -> none  [on_device(): spread = lax.all_gather(scaled, 'row', axis=2, tiled=True)]
where the time goes in v1:
time: 753 us; the launch traced here: 750 us
  waiting for transfers between devices  339 us (45%)
  blocking collectives  182 us (24%)
  local copies, waits for them, and re-layouts  116 us (15%)
  other arithmetic  62.1 us (8%)
  matrix products  34.7 us (5%)
  between operations  13.8 us (2%)
    unnamed x10, waiting for transfers between devices  127 us
    reduce_scatter x2, waiting for transfers between devices, on_device(): lax.psum_scatter(partial_in.astype(jnp.bfloat16), 'row', scatter_dimensio...  124 us
    reduce_scatter x4, waiting for transfers between devices, on_device(): lax.psum_scatter(partial_out.astype(jnp.bfloat16), 'col', scatter_dimensi...  78.6 us
    all_gather x2, blocking collectives, on_device(): image_panel = lax.all_gather(pieces, 'row', axis=2, tiled=True)  63.3 us
    unnamed x24, local copies, waits for them, and re-layouts  49.6 us
    all_to_all x2, blocking collectives, on_device(): lax.all_to_all(jnp.stack([scaled] * lax.axis_size('row')), 'row', 0, 0)  39.2 us
    another operation x7, other arithmetic, on_device(): factor = jnp.linalg.cholesky(gram_sum / WIDTH)  23.8 us
    all_to_all x2, blocking collectives, on_device(): lax.all_to_all(spread, 'col', split_axis=2, concat_axis=1, tiled=True)  22.4 us
  transfers between devices with their start and end apart: 9, of which 9 were waited for; matrix products, arithmetic and copies ran while one was open for 0% of the time, Pallas kernels for 0%

profile of v1, /device:TPU:0, one launch (start us, length us, event | category | flops | bytes accessed | tf_op | source)
XLA Modules:
  0.0 750.4 jit_solution(4201843655188856507)
XLA Ops:
  6.5 1.0 copy-done
  7.6 4.4 fusion.40
  12.1 22.8 %reduce-scatter.13.cloned.1.call-done = bf16[2,16,1024]{2,1,0:T(8,128)(2,1)} async-done(((bf16[2,64,1024]{2,1,0:T(8,128)(2,1)}), bf16[2,16,1024]{2,1,0:T(8,128)(2,1)}) %reduce-scatter.13.cloned.1.call-update) | async-done | bytes 65552 | tf_op jit(solution)/shard_map/reduce_scatter | solution.py:22
  34.9 0.9 multiply_convert_fusion.7
  35.9 19.6 %all_to_all.64 = bf16[8,2,16,1024]{3,2,1,0:T(8,128)(2,1)S(1)} all-to-all(bf16[8,2,16,1024]{3,2,1,0:T(8,128)(2,1)S(1)} %stack.4), channel_id=1, replica_groups=mesh['row'=8,'col'=4] {'row'}, dimensions={0} | all-to-all | bytes 1048576 | tf_op jit(solution)/shard_map/all_to_all | solution.py:28
  55.4 7.2 copy.73
  62.7 5.8 reshape.43
  68.4 11.2 %all_to_all.65 = bf16[4,2,32768]{2,1,0:T(2,128)(2,1)S(1)} all-to-all(bf16[4,2,32768]{2,1,0:T(2,128)(2,1)S(1)} %reshape.43), channel_id=1, replica_groups=mesh['row'=8,'col'=4] {'col'}, dimensions={0} | all-to-all | bytes 1048576 | tf_op jit(solution)/shard_map/all_to_all | solution.py:30
  79.6 4.1 reshape.44
  83.8 9.7 %copy.74 = bf16[2,16,4,2048]{3,2,1,0:T(4,128)(2,1)S(1)} copy(bf16[2,16,4,2048]{1,0,3,2:T(2,128)(2,1)} %bitcast.109) | data formatting | bytes 1048576 | tf_op jit(solution)/shard_map/all_to_all | solution.py:30
  93.7 4.4 fusion.46
  98.3 18.3 %reduce-scatter.15.cloned.1.call-done = bf16[2,16,1024]{2,1,0:T(8,128)(2,1)} async-done(((bf16[2,64,1024]{2,1,0:T(8,128)(2,1)}), bf16[2,16,1024]{2,1,0:T(8,128)(2,1)}) %reduce-scatter.15.cloned.1.call-update) | async-done | bytes 65552 | tf_op jit(solution)/shard_map/reduce_scatter | solution.py:22
  116.6 0.9 multiply_convert_fusion.6
  117.4 5.8 all_gather.18
  123.2 2.9 fusion.34
  126.7 1.0 copy.85
  127.6 63.2 %reduce-scatter.25.cloned.1.call-done = bf16[8,4096]{1,0:T(8,128)(2,1)} async-done(((bf16[64,4096]{1,0:T(8,128)(2,1)}), bf16[8,4096]{1,0:T(8,128)(2,1)}) %reduce-scatter.25.cloned.1.call-update) | async-done | bytes 65552
  190.9 0.9 reshape.40
  191.8 5.8 all_gather.19
  197.6 6.7 copy.55
  204.2 6.4 reshape.45
  210.6 3.6 all-to-all-start.2
  214.7 9.0 %all-to-all-done.2 = bf16[8,2,8192]{2,1,0:T(2,128)(2,1)S(1)} async-done(((bf16[8,2,8192]{2,1,0:T(2,128)(2,1)}), bf16[8,2,8192]{2,1,0:T(2,128)(2,1)S(1)}, u32[]{:S(2)}, u32[]{:S(2)}) %all-to-all-start.2) | async-done | bytes 262176 | tf_op jit(solution)/shard_map/all_to_all | solution.py:49
  223.7 5.9 reshape.46
  229.6 7.5 %fusion.2 = bf16[2,8,8,1024]{2,0,3,1:T(2,128)(2,1)} fusion(bf16[2,8,8,1024]{1,0,3,2:T(2,128)(2,1)} %bitcast.114, f32[2,1024]{0,1:T(8,128)S(1)} %copy.50), kind=kLoop, calls=%fused_computation.4 | loop fusion | flops 393216 | bytes 532480 | tf_op jit(solution)/shard_map/convert_element_type | solution.py:35
  237.2 8.9 %copy.56 = bf16[2,8,8,1024]{3,2,1,0:T(8,128)(2,1)S(1)} copy(bf16[2,8,8,1024]{2,0,3,1:T(2,128)(2,1)} %fusion.2) | data formatting | bytes 524288 | tf_op jit(solution)/shard_map/convert_element_type | solution.py:35
  246.0 3.7 fusion.28
  249.9 62.1 %reduce-scatter.17.cloned.1.call-done = bf16[2,64,256]{2,1,0:T(8,128)(2,1)} async-done(((bf16[2,64,2048]{2,1,0:T(8,128)(2,1)}), bf16[2,64,256]{2,1,0:T(8,128)(2,1)}) %reduce-scatter.17.cloned.1.call-update) | async-done | bytes 65552 | tf_op jit(solution)/shard_map/reduce_scatter | solution.py:40
  312.0 31.7 %all_gather.20 = bf16[2,64,2048]{2,1,0:T(8,128)(2,1)S(1)} all-gather(bf16[2,64,256]{2,1,0:T(8,128)(2,1)} %reduce-scatter.17.cloned.1.call-done), channel_id=1, replica_groups=mesh['row'=8,'col'=4] {'row'}, dimensions={2}, use_global_device_ids=true | all-gather | bytes 589824 | tf_op jit(solution)/shard_map/all_gather | solution.py:43
  343.9 10.3 %psum.14 = bf16[2,64,64]{1,2,0:T(8,128)(2,1)S(1)} all-reduce(bf16[2,64,64]{1,2,0:T(8,128)(2,1)S(1)} %convolution_convert_fusion.2), channel_id=1, replica_groups=mesh['row'=8,'col'=4] {'col'}, use_global_device_ids=true, to_apply=%region_4.0 | all-reduce | flops 8192 | bytes 32768 | tf_op jit(solution)/shard_map/psum | solution.py:53
  354.3 11.7 %custom-call.8 = f32[2,64,64]{2,1,0:T(8,128)S(1)} custom-call(f32[2,64,64]{2,1,0:T(8,128)S(1)} %fusion.62), custom_call_target="Cholesky" | custom-call | tf_op jit(solution)/shard_map/jit(cholesky)/cholesky | solution.py:54
  366.3 9.8 %custom-call.9 = f32[2,1,64,64]{2,3,1,0:T(8,128)S(1)} custom-call(f32[2,1,64,64]{3,2,1,0:T(8,128)S(1)} %select_bitcast_fusion.1), custom_call_target="InvertDiagBlocksLowerTriangular" | custom-call | tf_op jit(solution)/shard_map/vmap(jit(_solve_triangular))/triangular_solve | solution.py:55
  376.1 1.1 convolution_convert_fusion
  377.2 4.4 fusion.43
  381.7 19.2 %reduce-scatter.19.cloned.1.call-done = bf16[2,16,1024]{2,1,0:T(8,128)(2,1)} async-done(((bf16[2,64,1024]{2,1,0:T(8,128)(2,1)}), bf16[2,16,1024]{2,1,0:T(8,128)(2,1)}) %reduce-scatter.19.cloned.1.call-update) | async-done | bytes 65552 | tf_op jit(solution)/shard_map/reduce_scatter | solution.py:22
  400.9 0.9 multiply_convert_fusion.5
  401.9 19.6 %all_to_all.66 = bf16[8,2,16,1024]{3,2,1,0:T(8,128)(2,1)S(1)} all-to-all(bf16[8,2,16,1024]{3,2,1,0:T(8,128)(2,1)S(1)} %stack.5), channel_id=1, replica_groups=mesh['row'=8,'col'=4] {'row'}, dimensions={0} | all-to-all | bytes 1048576 | tf_op jit(solution)/shard_map/all_to_all | solution.py:28
  421.4 7.2 copy.75
  428.7 5.8 reshape.47
  434.4 11.2 %all_to_all.67 = bf16[4,2,32768]{2,1,0:T(2,128)(2,1)S(1)} all-to-all(bf16[4,2,32768]{2,1,0:T(2,128)(2,1)S(1)} %reshape.47), channel_id=1, replica_groups=mesh['row'=8,'col'=4] {'col'}, dimensions={0} | all-to-all | bytes 1048576 | tf_op jit(solution)/shard_map/all_to_all | solution.py:30
  445.7 4.1 reshape.48
  449.8 9.7 %copy.76 = bf16[2,16,4,2048]{3,2,1,0:T(4,128)(2,1)S(1)} copy(bf16[2,16,4,2048]{1,0,3,2:T(2,128)(2,1)} %bitcast.111) | data formatting | bytes 1048576 | tf_op jit(solution)/shard_map/all_to_all | solution.py:30
  459.8 4.4 fusion.49
  464.3 18.3 %reduce-scatter.21.cloned.1.call-done = bf16[2,16,1024]{2,1,0:T(8,128)(2,1)} async-done(((bf16[2,64,1024]{2,1,0:T(8,128)(2,1)}), bf16[2,16,1024]{2,1,0:T(8,128)(2,1)}) %reduce-scatter.21.cloned.1.call-update) | async-done | bytes 65552 | tf_op jit(solution)/shard_map/reduce_scatter | solution.py:22
  482.5 0.9 multiply_convert_fusion.4
  483.4 5.8 all_gather.21
  489.2 2.9 fusion.37
  492.6 1.0 copy.86
  493.7 63.2 %reduce-scatter.27.cloned.1.call-done = bf16[8,4096]{1,0:T(8,128)(2,1)} async-done(((bf16[64,4096]{1,0:T(8,128)(2,1)}), bf16[8,4096]{1,0:T(8,128)(2,1)}) %reduce-scatter.27.cloned.1.call-update) | async-done | bytes 65552
  556.9 0.9 reshape.42
  557.8 5.8 all_gather.22
  563.5 6.7 copy.64
  570.2 5.8 reshape.49
  576.0 12.8 %all_to_all.68 = bf16[8,2,8192]{2,1,0:T(2,128)(2,1)S(1)} all-to-all(bf16[8,2,8192]{2,1,0:T(2,128)(2,1)S(1)} %reshape.49), channel_id=1, replica_groups=mesh['row'=8,'col'=4] {'row'}, dimensions={0} | all-to-all | bytes 524288 | tf_op jit(solution)/shard_map/all_to_all | solution.py:49
  588.8 5.9 reshape.50
  594.7 7.5 %fusion.3 = bf16[2,8,8,1024]{2,0,3,1:T(2,128)(2,1)} fusion(bf16[2,8,8,1024]{1,0,3,2:T(2,128)(2,1)} %bitcast.112, f32[2,1024]{0,1:T(8,128)S(1)} %copy.50), kind=kLoop, calls=%fused_computation.5 | loop fusion | flops 393216 | bytes 532480 | tf_op jit(solution)/shard_map/convert_element_type | solution.py:35
  602.2 8.9 %copy.65 = bf16[2,8,8,1024]{3,2,1,0:T(8,128)(2,1)S(1)} copy(bf16[2,8,8,1024]{2,0,3,1:T(2,128)(2,1)} %fusion.3) | data formatting | bytes 524288 | tf_op jit(solution)/shard_map/convert_element_type | solution.py:35
  611.1 3.8 fusion.31
  614.9 62.2 %reduce-scatter.23.cloned.1.call-done = bf16[2,64,256]{2,1,0:T(8,128)(2,1)} async-done(((bf16[2,64,2048]{2,1,0:T(8,128)(2,1)}), bf16[2,64,256]{2,1,0:T(8,128)(2,1)}) %reduce-scatter.23.cloned.1.call-update) | async-done | bytes 65552 | tf_op jit(solution)/shard_map/reduce_scatter | solution.py:40
  677.1 31.6 %all_gather.23 = bf16[2,64,2048]{2,1,0:T(8,128)(2,1)S(1)} all-gather(bf16[2,64,256]{2,1,0:T(8,128)(2,1)} %reduce-scatter.23.cloned.1.call-done), channel_id=1, replica_groups=mesh['row'=8,'col'=4] {'row'}, dimensions={2}, use_global_device_ids=true | all-gather | bytes 589824 | tf_op jit(solution)/shard_map/all_gather | solution.py:43
  709.1 10.5 %psum.15 = bf16[2,64,64]{1,2,0:T(8,128)(2,1)S(1)} all-reduce(bf16[2,64,64]{1,2,0:T(8,128)(2,1)S(1)} %convolution_convert_fusion.1), channel_id=1, replica_groups=mesh['row'=8,'col'=4] {'col'}, use_global_device_ids=true, to_apply=%region_11.14 | all-reduce | flops 8192 | bytes 32768 | tf_op jit(solution)/shard_map/psum | solution.py:53
  719.7 11.7 %custom-call.10 = f32[2,64,64]{2,1,0:T(8,128)S(1)} custom-call(f32[2,64,64]{2,1,0:T(8,128)S(1)} %fusion.60), custom_call_target="Cholesky" | custom-call | tf_op jit(solution)/shard_map/jit(cholesky)/cholesky | solution.py:54
  731.7 9.8 %custom-call.11 = f32[2,1,64,64]{2,3,1,0:T(8,128)S(1)} custom-call(f32[2,1,64,64]{3,2,1,0:T(8,128)S(1)} %select_bitcast_fusion), custom_call_target="InvertDiagBlocksLowerTriangular" | custom-call | tf_op jit(solution)/shard_map/vmap(jit(_solve_triangular))/triangular_solve | solution.py:55
  741.5 2.0 fusion.52
  (50 shorter events, 3.9 us)
Async XLA Ops:
  6.5 1.0 copy-start
  6.5 5.5 copy-start.2
  6.5 28.4 %reduce-scatter.13.cloned.1.call-start = ((), (), s32[]{:S(2)}) async-start(), calls=%async_computation.14 | async-start | bytes 327680 | tf_op jit(solution)/shard_map/reduce_scatter | solution.py:22
  12.0 104.5 %reduce-scatter.15.cloned.1.call-start = ((), (), s32[]{:S(2)}) async-start(), calls=%async_computation.15 | async-start | bytes 327680 | tf_op jit(solution)/shard_map/reduce_scatter | solution.py:22
  98.2 92.7 %reduce-scatter.25.cloned.1.call-start = ((), (), s32[]{:S(2)}) async-start(), calls=%async_computation.20 | async-start | bytes 589824
  210.6 13.1 %all-to-all-start.2 = ((bf16[8,2,8192]{2,1,0:T(2,128)(2,1)}), bf16[8,2,8192]{2,1,0:T(2,128)(2,1)S(1)}, u32[]{:S(2)}, u32[]{:S(2)}) async-start(bf16[8,2,8192]{2,1,0:T(2,128)(2,1)} %reshape.45), calls=%async_computation.4 | async-start | bytes 524288 | tf_op jit(solution)/shard_map/all_to_all | solution.py:49
  214.2 97.7 %reduce-scatter.17.cloned.1.call-start = ((), (), s32[]{:S(2)}) async-start(), calls=%async_computation.16 | async-start | bytes 589824 | tf_op jit(solution)/shard_map/reduce_scatter | solution.py:40
  249.8 151.2 %reduce-scatter.19.cloned.1.call-start = ((), (), s32[]{:S(2)}) async-start(), calls=%async_computation.17 | async-start | bytes 327680 | tf_op jit(solution)/shard_map/reduce_scatter | solution.py:22
  381.6 100.9 %reduce-scatter.21.cloned.1.call-start = ((), (), s32[]{:S(2)}) async-start(), calls=%async_computation.18 | async-start | bytes 327680 | tf_op jit(solution)/shard_map/reduce_scatter | solution.py:22
  464.2 92.6 %reduce-scatter.27.cloned.1.call-start = ((), (), s32[]{:S(2)}) async-start(), calls=%async_computation.21 | async-start | bytes 589824
  493.6 183.5 %reduce-scatter.23.cloned.1.call-start = ((), (), s32[]{:S(2)}) async-start(), calls=%async_computation.19 | async-start | bytes 589824 | tf_op jit(solution)/shard_map/reduce_scatter | solution.py:40
  611.1 132.4 %copy-start.1 = (bf16[2,64,2048]{2,1,0:T(8,128)(2,1)S(1)}, bf16[2,64,2048]{2,1,0:T(8,128)(2,1)}, u32[]{:S(2)}) copy-start(bf16[2,64,2048]{2,1,0:T(8,128)(2,1)} %param.8) | copy-start | bytes 1572868
Sparse Core Ops, SparseCore 0:
  12.1 22.7 reduce-scatter.12
  98.3 18.1 reduce-scatter.14
  127.8 63.0 reduce-scatter.24
  249.9 62.0 reduce-scatter.16
  381.8 19.1 reduce-scatter.18
  464.3 18.1 reduce-scatter.20
  493.7 63.0 reduce-scatter.26
  615.0 62.0 reduce-scatter.22
